TPU v7x, 32 devices: a whole 2x2x4 slice. The times are simulated.
32 devices in a mesh: dp: 8 (over z, x), seq: 4 (over y, core).
Axes of the slice: x: 2, y: 2, z: 4, core: 2. Of those that a mesh axis runs over, the one named last changes fastest.
Arguments:
- tokens: bfloat16 [8, 1024, 1600], P('dp', 'seq'), may hold values from -6 to 6
- cotangent: bfloat16 [8, 1024, 1600], P('dp', 'seq'), may hold values from -6 to 6
- lengths: int32 [8], P('dp'), may hold values from 256 to 1024, as said below
- w_qkv: bfloat16 [7680000], P(('dp', 'seq')), may hold values from -0.15625 to 0.15625
- w_out: bfloat16 [2560000], P(('dp', 'seq')), may hold values from -2.5 to 2.5
- w_fc: bfloat16 [10246400], P(('dp', 'seq')), may hold values from -0.15625 to 0.15625
- w_proj: bfloat16 [10240000], P(('dp', 'seq')), may hold values from -0.078125 to 0.078125
- attention_vectors: bfloat16 [6400], P(('dp', 'seq')), as said below
- block_vectors: bfloat16 [6400], P(('dp', 'seq')), as said below
Outputs:
- output: bfloat16 [8, 1024, 1600], P('dp', 'seq')
- input_grad: float32 [8, 1024, 1600], P('dp', 'seq')
- grad_qkv: float32 [7680000], P(('dp', 'seq'))
- grad_out: float32 [2560000], P(('dp', 'seq'))
- grad_fc: float32 [10246400], P(('dp', 'seq'))
- grad_proj: float32 [10240000], P(('dp', 'seq'))
- grad_attention_vectors: float32 [6400], P(('dp', 'seq'))
- grad_block_vectors: float32 [6400], P(('dp', 'seq'))
Inputs may be any that keep to these rules, and one draw needn't show every extreme that they name: `lengths`: valid positions of each slot; in every draw one slot has all 1024 and one has 256. `attention_vectors`: gains near one, biases of order one half. `block_vectors`: gains near one, biases of order one half.
All inputs are finite; a program needn't handle non-finite values.
Results may differ from a plain program's by a relative error of at most 0.01.
Values may be sent and summed in bfloat16 or wider, within the bound.
No kernel may reach another device: no remote copies, remote signals or barrier semaphores. Data moves between devices by JAX's collectives and lax.ppermute only.
A program may use at most 448 MiB of HBM per device.

v0:
```python
from functools import partial
import jax
import jax.numpy as jnp
from jax import lax
from jax.sharding import PartitionSpec as P

HD = 64
EPS = 1e-05


def layer_norm(value, gain, shift):
    centre = value - jnp.mean(value, axis=-1, keepdims=True)
    spread = jnp.mean(centre * centre, axis=-1, keepdims=True)
    return centre * lax.rsqrt(spread + EPS) * gain + shift


def tanh_gelu(value):
    return jax.nn.gelu(value, approximate=True)


def split_weights(gathered, width):
    flat_qkv, flat_out, flat_fc, flat_proj, first_vectors, second_vectors = gathered
    hidden = flat_fc.shape[0] // (width + 1)
    expand_full = flat_fc.reshape(width + 1, hidden)
    token_rows = (
        jnp.concatenate([first_vectors, second_vectors]).astype(jnp.float32).reshape(8, width)
    )
    expand_bias = expand_full[width].astype(jnp.float32)
    return (
        flat_qkv.reshape(width, 3 * width),
        flat_out.reshape(width, width),
        expand_full[:width],
        flat_proj.reshape(hidden, width),
        token_rows,
        expand_bias,
    )


def to_heads(value, heads):
    slots, count, width = value.shape
    return jnp.moveaxis(value.reshape(slots, count, heads, width // heads), 2, 0)


def from_heads(value):
    heads, slots, count, size = value.shape
    return jnp.moveaxis(value, 0, 2).reshape(slots, count, heads * size)


def head_scores(allowed, query, keys):
    scores = jnp.einsum("sqd,skd->sqk", query, keys, preferred_element_type=jnp.float32) * 0.125
    return jnp.where(allowed, scores, -1e30)


def head_forward(allowed, item):
    query, keys, values = item
    scores = head_scores(allowed, query, keys)
    peak = jnp.max(scores, axis=-1, keepdims=True)
    raised = jnp.exp(scores - peak)
    total = jnp.sum(raised, axis=-1, keepdims=True)
    weights = (raised / total).astype(jnp.bfloat16)
    result = jnp.einsum("sqk,skd->sqd", weights, values, preferred_element_type=jnp.float32)
    return (result, (peak + jnp.log(total))[..., 0])


def head_backward(allowed, item):
    query, keys, values, grad_result, normal = item
    scores = head_scores(allowed, query, keys)
    probs = jnp.where(allowed, jnp.exp(scores - normal[..., None]), 0.0)
    weights = probs.astype(jnp.bfloat16)
    grad_probs = jnp.einsum("sqd,skd->sqk", grad_result, values, preferred_element_type=jnp.float32)
    inner_total = jnp.sum(probs * grad_probs, axis=-1, keepdims=True)
    grad_scores = (probs * (grad_probs - inner_total) * 0.125).astype(jnp.bfloat16)
    grad_query = jnp.einsum("sqk,skd->sqd", grad_scores, keys, preferred_element_type=jnp.float32)
    grad_keys = jnp.einsum("sqk,sqd->skd", grad_scores, query, preferred_element_type=jnp.float32)
    grad_values = jnp.einsum(
        "sqk,sqd->skd", weights, grad_result, preferred_element_type=jnp.float32
    )
    return (grad_query, grad_keys, grad_values)


def local(tokens, cotangent, lengths, w_qkv, w_out, w_fc, w_proj, attention_vectors, block_vectors):
    slots, count, width = tokens.shape
    heads = width // HD
    rank = lax.axis_index("seq")
    span = count * lax.axis_size("seq")
    part_qkv, part_out, part_fc, part_proj, part_first, part_second = (
        lax.all_gather(w_qkv, "seq", axis=0, tiled=True),
        lax.all_gather(w_out, "seq", axis=0, tiled=True),
        lax.all_gather(w_fc, "seq", axis=0, tiled=True),
        lax.all_gather(w_proj, "seq", axis=0, tiled=True),
        lax.all_gather(attention_vectors, "seq", axis=0, tiled=True),
        lax.all_gather(block_vectors, "seq", axis=0, tiled=True),
    )
    gathered = (
        lax.all_gather(part_qkv, "dp", axis=0, tiled=True),
        lax.all_gather(part_out, "dp", axis=0, tiled=True),
        lax.all_gather(part_fc, "dp", axis=0, tiled=True),
        lax.all_gather(part_proj, "dp", axis=0, tiled=True),
        lax.all_gather(part_first, "dp", axis=0, tiled=True),
        lax.all_gather(part_second, "dp", axis=0, tiled=True),
    )
    (
        query_key_value_weight,
        output_weight,
        expand_weight,
        contract_weight,
        token_rows,
        expand_bias,
    ) = split_weights(gathered, width)
    place = rank * count + jnp.arange(count)
    key_place = jnp.arange(span)
    allowed = (key_place[None, None, :] <= place[None, :, None]) & (
        key_place[None, None, :] < lengths[:, None, None]
    )
    valid = place[None, :] < lengths[:, None]
    source = tokens.astype(jnp.float32)
    normed_low = layer_norm(source, token_rows[0], token_rows[1]).astype(jnp.bfloat16)
    mixed_heads = jnp.einsum(
        "scd,de->sce", normed_low, query_key_value_weight, preferred_element_type=jnp.float32
    )
    query = (mixed_heads[..., :width] + token_rows[2]).astype(jnp.bfloat16)
    keys = mixed_heads[..., width : 2 * width].astype(jnp.bfloat16)
    values = (mixed_heads[..., 2 * width :] + token_rows[3]).astype(jnp.bfloat16)
    all_keys, all_values = (
        lax.all_gather(keys, "seq", axis=1, tiled=True),
        lax.all_gather(values, "seq", axis=1, tiled=True),
    )
    query_heads = to_heads(query, heads)
    key_heads = to_heads(all_keys, heads)
    value_heads = to_heads(all_values, heads)
    head_result, normal = lax.map(
        partial(head_forward, allowed), (query_heads, key_heads, value_heads)
    )
    attention_output = from_heads(head_result).astype(jnp.bfloat16)
    middle_state = (
        source
        + jnp.einsum(
            "scd,de->sce", attention_output, output_weight, preferred_element_type=jnp.float32
        )
        + token_rows[4]
    )
    second_normed = layer_norm(middle_state, token_rows[5], token_rows[6]).astype(jnp.bfloat16)
    inner_hidden = (
        jnp.einsum("scd,df->scf", second_normed, expand_weight, preferred_element_type=jnp.float32)
        + expand_bias
    )
    active_low = tanh_gelu(inner_hidden).astype(jnp.bfloat16)
    result = (
        middle_state
        + jnp.einsum("scf,fd->scd", active_low, contract_weight, preferred_element_type=jnp.float32)
        + token_rows[7]
    )
    output = result.astype(jnp.bfloat16)
    again_qkv, again_out, again_fc, again_proj, again_first, again_second = (
        lax.all_gather(w_qkv, "seq", axis=0, tiled=True),
        lax.all_gather(w_out, "seq", axis=0, tiled=True),
        lax.all_gather(w_fc, "seq", axis=0, tiled=True),
        lax.all_gather(w_proj, "seq", axis=0, tiled=True),
        lax.all_gather(attention_vectors, "seq", axis=0, tiled=True),
        lax.all_gather(block_vectors, "seq", axis=0, tiled=True),
    )
    again = (
        lax.all_gather(again_qkv, "dp", axis=0, tiled=True),
        lax.all_gather(again_out, "dp", axis=0, tiled=True),
        lax.all_gather(again_fc, "dp", axis=0, tiled=True),
        lax.all_gather(again_proj, "dp", axis=0, tiled=True),
        lax.all_gather(again_first, "dp", axis=0, tiled=True),
        lax.all_gather(again_second, "dp", axis=0, tiled=True),
    )
    (
        query_key_value_weight,
        output_weight,
        expand_weight,
        contract_weight,
        token_rows,
        expand_bias,
    ) = split_weights(again, width)
    grad_result = cotangent * valid.astype(jnp.bfloat16)[..., None]
    grad_wide = grad_result.astype(jnp.float32)
    grad_proj = jnp.einsum(
        "scf,scd->fd", active_low, grad_result, preferred_element_type=jnp.float32
    )
    bias_proj_grad = jnp.sum(grad_wide, axis=(0, 1))
    grad_active = jnp.einsum(
        "scd,fd->scf", grad_result, contract_weight, preferred_element_type=jnp.float32
    )
    gelu_back = jax.vjp(tanh_gelu, inner_hidden)[1]
    inner_low = gelu_back(grad_active)[0].astype(jnp.bfloat16)
    bias_fc_grad = jnp.sum(inner_low.astype(jnp.float32), axis=(0, 1))
    grad_fc = jnp.einsum(
        "scd,scf->df", second_normed, inner_low, preferred_element_type=jnp.float32
    )
    grad_fc_full = jnp.concatenate([grad_fc, bias_fc_grad[None, :]], axis=0).reshape(-1)
    grad_normed_two = jnp.einsum(
        "scf,df->scd", inner_low, expand_weight, preferred_element_type=jnp.float32
    )
    norm_two_back = jax.vjp(layer_norm, middle_state, token_rows[5], token_rows[6])[1]
    grad_mid, gain_two_grad, shift_two_grad = norm_two_back(grad_normed_two)
    grad_mid = grad_mid + grad_wide
    branch_low = grad_mid.astype(jnp.bfloat16)
    bias_out_grad = jnp.sum(branch_low.astype(jnp.float32), axis=(0, 1))
    grad_out_mat = jnp.einsum(
        "scd,sce->de", attention_output, branch_low, preferred_element_type=jnp.float32
    )
    grad_attended = jnp.einsum(
        "sce,de->scd", branch_low, output_weight, preferred_element_type=jnp.float32
    ).astype(jnp.bfloat16)
    grad_query, grad_keys, grad_values = lax.map(
        partial(head_backward, allowed),
        (query_heads, key_heads, value_heads, to_heads(grad_attended, heads), normal),
    )
    keys_sum, values_sum = (
        lax.psum_scatter(from_heads(grad_keys), "seq", scatter_dimension=1, tiled=True),
        lax.psum_scatter(from_heads(grad_values), "seq", scatter_dimension=1, tiled=True),
    )
    query_low = from_heads(grad_query).astype(jnp.bfloat16)
    keys_low = keys_sum.astype(jnp.bfloat16)
    values_low = values_sum.astype(jnp.bfloat16)
    bias_query_grad = jnp.sum(query_low.astype(jnp.float32), axis=(0, 1))
    bias_value_grad = jnp.sum(values_low.astype(jnp.float32), axis=(0, 1))
    grad_mixed = jnp.concatenate([query_low, keys_low, values_low], axis=-1)
    grad_qkv = jnp.einsum("scd,sce->de", normed_low, grad_mixed, preferred_element_type=jnp.float32)
    grad_normed = jnp.einsum(
        "sce,de->scd", grad_mixed, query_key_value_weight, preferred_element_type=jnp.float32
    )
    norm_one_back = jax.vjp(layer_norm, source, token_rows[0], token_rows[1])[1]
    grad_source, gain_one_grad, shift_one_grad = norm_one_back(grad_normed)
    input_grad = grad_mid + grad_source
    first_grad = jnp.concatenate([gain_one_grad, shift_one_grad, bias_query_grad, bias_value_grad])
    second_grad = jnp.concatenate([bias_out_grad, gain_two_grad, shift_two_grad, bias_proj_grad])
    qkv_part, out_part, fc_part, proj_part, first_part, second_part = (
        lax.psum_scatter(grad_qkv.reshape(-1), "dp", scatter_dimension=0, tiled=True),
        lax.psum_scatter(grad_out_mat.reshape(-1), "dp", scatter_dimension=0, tiled=True),
        lax.psum_scatter(grad_fc_full, "dp", scatter_dimension=0, tiled=True),
        lax.psum_scatter(grad_proj.reshape(-1), "dp", scatter_dimension=0, tiled=True),
        lax.psum_scatter(first_grad, "dp", scatter_dimension=0, tiled=True),
        lax.psum_scatter(second_grad, "dp", scatter_dimension=0, tiled=True),
    )
    qkv_shard, out_shard, fc_shard, proj_shard, first_shard, second_shard = (
        lax.psum_scatter(qkv_part, "seq", scatter_dimension=0, tiled=True),
        lax.psum_scatter(out_part, "seq", scatter_dimension=0, tiled=True),
        lax.psum_scatter(fc_part, "seq", scatter_dimension=0, tiled=True),
        lax.psum_scatter(proj_part, "seq", scatter_dimension=0, tiled=True),
        lax.psum_scatter(first_part, "seq", scatter_dimension=0, tiled=True),
        lax.psum_scatter(second_part, "seq", scatter_dimension=0, tiled=True),
    )
    return (
        output,
        input_grad,
        qkv_shard,
        out_shard,
        fc_shard,
        proj_shard,
        first_shard,
        second_shard,
    )


def solution(mesh):
    in_specs = (
        P("dp", "seq", None),
        P("dp", "seq", None),
        P("dp"),
        P(("dp", "seq")),
        P(("dp", "seq")),
        P(("dp", "seq")),
        P(("dp", "seq")),
        P(("dp", "seq")),
        P(("dp", "seq")),
    )
    out_specs = (
        P("dp", "seq", None),
        P("dp", "seq", None),
        P(("dp", "seq")),
        P(("dp", "seq")),
        P(("dp", "seq")),
        P(("dp", "seq")),
        P(("dp", "seq")),
        P(("dp", "seq")),
    )
    return jax.shard_map(local, mesh=mesh, in_specs=in_specs, out_specs=out_specs, check_vma=False)
```

profile of v0, /device:TPU:0, one launch (start us, length us, event | category | flops | bytes accessed | tf_op | source)
XLA Modules:
  0.0 6387.4 jit_solution(10073918586808207974)
XLA Ops:
  23.4 25.4 all-gather.19.cloned.1.call-done
  57.3 19.0 all-gather.2
  77.1 40.4 all-reduce.29.cloned.1.call-done
  124.8 39.2 dynamic-update-slice.5
  172.5 51.9 all-reduce.22
  226.2 478.7 %all-gather.21.cloned.1.call-done = bf16[8,1,960000]{2,1,0:T(2,128)(2,1)} async-done(((bf16[1,1,960000]{2,1,0:T(2,128)(2,1)}), bf16[8,1,960000]{2,1,0:T(2,128)(2,1)}) %all-gather.21.cloned.1.call-update) | async-done | bytes 15360016 | tf_op jit(solution)/shard_map/all_gather | solution.py:95
  704.9 325.4 %reduce.24 = bf16[8,960000]{1,0:T(8,128)(2,1)} reduce(bf16[8,1,960000]{2,1,0:T(2,128)(2,1)} %all-gather.21.cloned.1.call-done, bf16[]{:T(256)} %constant.172), dimensions={1}, to_apply=%all-gather.1.reduce_sub_computation | reduce | bytes 30720002 | tf_op jit(solution)/shard_map/all_gather | solution.py:95
  1030.3 34.2 reshape.626
  1064.5 25.2 reshape.541
  1133.1 32.0 reduce.25
  1187.1 325.9 %all-reduce.31.cloned.1.call-done = bf16[10246400]{0:T(1024)(128)(2,1)} async-done(((bf16[10246400]{0:T(1024)(128)(2,1)}), bf16[10246400]{0:T(1024)(128)(2,1)}) %all-reduce.31.cloned.1.call-update) | async-done | bytes 20492816
  1530.0 35.4 slice.74
  1583.3 79.7 %while.28 = (s32[]{:T(128)}, bf16[25,1,256,64]{2,3,1,0:T(8,128)(2,1)S(1)}, f32[25,1,256]{2,1,0:T(1,128)S(1)}, bf16[25,1,256,64]{3,2,1,0:T(8,128)(2,1)}, bf16[25,...) while((s32[]{:T(128)}, ...), condition=%wide.region_5.6_spmd.clone, body=%wide.region_2.5_spmd.clone.sunk | while | flops 69730048 | bytes 3815529 | solution.py:131
  1681.0 289.2 %all-gather.17.cloned.1.call-done = bf16[10240000]{0:T(1024)(128)(2,1)} async-done(((bf16[1280000]{0:T(1024)(128)(2,1)}), bf16[10240000]{0:T(1024)(128)(2,1)}) %all-gather.17.cloned.1.call-update) | async-done | bytes 20480016 | tf_op jit(solution)/shard_map/all_gather | solution.py:98
  1970.3 34.0 reshape.547
  2039.8 200.8 %while.29 = (s32[]{:T(128)}, bf16[25,1,256,64]{2,3,1,0:T(8,128)(2,1)S(1)}, f32[25,1,1024,64]{2,3,1,0:T(8,128)}, f32[25,1,1024,64]{2,3,1,0:T(8,128)}, bf16[25,1,2...) while((s32[]{:T(128)}, ...), condition=%wide.region_12.13_spmd.clone, body=%wide.region_10.12_spmd.clone.sunk | while | flops 171179776 | bytes 9515137 | solution.py:208
  2241.4 22.7 fusion.84
  2264.1 48.3 reshape.557
  2351.2 28.1 pad_maximum_fusion
  2379.3 39.9 reshape.556
  2438.2 36.5 reshape.554
  2477.1 3609.6 %all-reduce.33.cloned.1.call-done = (f32[7680000]{0:T(1024)}, f32[2560000]{0:T(1024)}, f32[10246400]{0:T(1024)}, f32[10240000]{0:T(1024)}) async-done(((f32[7680000]{0:T(1024)}, f32[2560000]{0:T(1024)}, f32[10246400]{0:T(1024)}, f32[10240000]{0:T(1024)}), (f32[7680000]{0:T(1024)}, f32[2560000]{0:T(1024)}, f32[10246400]{0:T(1024)}, f32[10240000]{0:T(1024)})) %all-reduce.33.cloned.1.call-update) | async-done | bytes 122905616
  6137.3 35.6 all-reduce.18
  6184.1 186.5 %all-reduce.35.cloned.1.call-done = (f32[960000]{0:T(1024)}, f32[320000]{0:T(1024)}, f32[1280800]{0:T(1024)}, f32[1280000]{0:T(1024)}) async-done(((f32[960000]{0:T(1024)}, f32[320000]{0:T(1024)}, f32[1280800]{0:T(1024)}, f32[1280000]{0:T(1024)}), (f32[960000]{0:T(1024)}, f32[320000]{0:T(1024)}, f32[1280800]{0:T(1024)}, f32[1280000]{0:T(1024)})) %all-reduce.35.cloned.1.call-update) | async-done | bytes 15363216
  (489 shorter events, 598.5 us)
Async XLA Ops:
  7.2 41.7 all-gather.19.cloned.1.call-start
  13.5 103.9 %all-reduce.29.cloned.1.call-start = ((), (), s32[]{:S(2)}) async-start(), calls=%async_computation.7 | async-start | bytes 5124096
  23.4 681.5 %all-gather.21.cloned.1.call-start = ((), (), s32[]{:S(2)}) async-start(), calls=%async_computation.10 | async-start | bytes 34560000 | tf_op jit(solution)/shard_map/all_gather | solution.py:95
  48.9 1061.5 %all-gather.25.cloned.1.call-start = ((), (), s32[]{:S(2)}) async-start(), calls=%async_computation.12 | async-start | bytes 6400000 | tf_op jit(solution)/shard_map/all_gather | solution.py:90
  57.1 1076.1 %all-gather.23.cloned.1.call-start = ((), (), s32[]{:S(2)}) async-start(), calls=%async_computation.11 | async-start | bytes 11520000 | tf_op jit(solution)/shard_map/all_gather | solution.py:96
  76.4 1436.7 %all-reduce.31.cloned.1.call-start = ((), (), s32[]{:S(2)}) async-start(), calls=%async_computation.8 | async-start | bytes 40988672
  164.0 60.4 copy-start
  164.0 1403.9 %all-gather.13.cloned.1.call-start = ((), (), s32[]{:S(2)}) async-start(), calls=%async_computation.2 | async-start | bytes 4096000 | tf_op jit(solution)/shard_map/all_gather | solution.py:125
  224.6 865.1 %copy-start.19 = (f32[256]{0:T(256)}, f32[256]{0:T(256)S(1)}, u32[]{:S(2)}) copy-start(f32[256]{0:T(256)S(1)} %broadcast_multiply_fusion.1) | copy-start | bytes 3076
  224.9 864.8 %copy-start.21 = (f32[256]{0:T(256)}, f32[256]{0:T(256)S(1)}, u32[]{:S(2)}) copy-start(f32[256]{0:T(256)S(1)} %fusion.95) | copy-start | bytes 3076
  226.2 863.5 %copy-start.14 = (f32[1600]{0:T(1024)}, f32[1600]{0:T(1024)S(1)}, u32[]{:S(2)}) copy-start(f32[1600]{0:T(1024)S(1)} %get-tuple-element.229) | copy-start | bytes 19204
  226.2 863.6 %copy-start.17 = (f32[1600]{0:T(1024)}, f32[1600]{0:T(1024)S(1)}, u32[]{:S(2)}) copy-start(f32[1600]{0:T(1024)S(1)} %get-tuple-element.228) | copy-start | bytes 19204
  1107.0 469.1 %all-gather.15.cloned.1.call-start = ((), (), s32[]{:S(2)}) async-start(), calls=%async_computation.3 | async-start | bytes 4096000 | tf_op jit(solution)/shard_map/all_gather | solution.py:126
  1110.4 859.9 %all-gather.17.cloned.1.call-start = ((), (), s32[]{:S(2)}) async-start(), calls=%async_computation.4 | async-start | bytes 23040000 | tf_op jit(solution)/shard_map/all_gather | solution.py:98
  1132.3 1286.9 %reduce-scatter.3.cloned.1.call-start = ((), (), s32[]{:S(2)}) async-start(), calls=%async_computation.5 | async-start | bytes 8192000 | tf_op jit(solution)/shard_map/reduce_scatter | solution.py:213
  1133.1 1108.3 %copy-start.31 = (bf16[256]{0:T(256)(128)(2,1)}, bf16[256]{0:T(256)(128)(2,1)S(1)}, u32[]{:S(2)}) copy-start(bf16[256]{0:T(256)(128)(2,1)S(1)} %compare_convert_fusion) | copy-start | bytes 1540
  1681.0 323.2 %copy-start.4 = (bf16[1,256,1600]{1,2,0:T(8,128)(2,1)S(1)}, bf16[1,256,1600]{1,2,0:T(8,128)(2,1)}, u32[]{:S(2)}) copy-start(bf16[1,256,1600]{1,2,0:T(8,128)(2,1)} %param.14) | copy-start | bytes 2457604
  2240.6 181.1 %reduce-scatter.5.cloned.1.call-start = ((), (), s32[]{:S(2)}) async-start(), calls=%async_computation.6 | async-start | bytes 8192000 | tf_op jit(solution)/shard_map/reduce_scatter | solution.py:214
  2241.3 3845.4 %all-reduce.33.cloned.1.call-start = ((), (), s32[]{:S(2)}) async-start(), calls=%async_computation.13 | async-start | bytes 245817344
  2264.1 48.3 copy-start.8
  2474.8 3895.8 %all-reduce.35.cloned.1.call-start = ((), (), s32[]{:S(2)}) async-start(), calls=%async_computation.14 | async-start | bytes 30736384
  6136.0 44.8 copy-start.5
  6136.0 44.8 copy-start.26
  6136.1 44.7 copy-start.32
  (24 other events, 141.8 us)
Sparse Core Ops, SparseCore 0:
  13.6 35.2 all-gather.18
  51.3 66.0 all-reduce.28
  119.0 585.7 all-gather.20
  706.9 39.7 all-gather.24
  749.0 147.8 all-gather.22
  901.4 611.6 all-reduce.30
  1515.3 28.8 all-gather.12
  1546.3 29.6 all-gather.14
  1577.7 392.5 all-gather.16
  2240.7 60.0 reduce-scatter.2
  2303.4 60.0 reduce-scatter.4
  2474.9 3611.7 all-reduce.32
  6103.9 266.6 all-reduce.34
where the time goes:
time: 6410 us; the launch traced here: 6390 us
  waiting for transfers between devices  4960 us (77%)
  other arithmetic  434 us (7%)
  local copies, waits for them, and re-layouts  433 us (7%)
  matrix products  418 us (7%)
  blocking collectives  119 us (2%)
    unnamed x17, waiting for transfers between devices  4160 us
    all_gather x1, waiting for transfers between devices, local(): lax.all_gather(part_qkv, 'dp', axis=0, tiled=True)  479 us
    all_gather x1, other arithmetic, local(): lax.all_gather(part_qkv, 'dp', axis=0, tiled=True)  325 us
    all_gather x1, waiting for transfers between devices, local(): lax.all_gather(part_proj, 'dp', axis=0, tiled=True)  289 us
    unnamed x101, local copies, waits for them, and re-layouts  152 us
  transfers between devices with their start and end apart: 13, of which 8 were waited for; matrix products, arithmetic and copies ran while one was open for 15% of the time, Pallas kernels for 0%

commit v1 on v0

--- a/solution.py
+++ b/solution.py
@@ -6,6 +6,18 @@
 
 HD = 64
 EPS = 1e-05
+
+
+def gather_by_bits(x, axis, dim):
+    ways, here = (lax.axis_size(axis), lax.axis_index(axis))
+    grown, reach = (x, 1)
+    while reach < ways:
+        theirs = lax.ppermute(grown, axis, [(d, d ^ reach) for d in range(ways)])
+        mine_first = jnp.concatenate([grown, theirs], axis=dim)
+        theirs_first = jnp.concatenate([theirs, grown], axis=dim)
+        grown = jnp.where(here & reach == 0, mine_first, theirs_first)
+        reach = 2 * reach
+    return grown
 
 
 def layer_norm(value, gain, shift):
@@ -92,7 +104,7 @@
         lax.all_gather(block_vectors, "seq", axis=0, tiled=True),
     )
     gathered = (
-        lax.all_gather(part_qkv, "dp", axis=0, tiled=True),
+        gather_by_bits(part_qkv, "dp", 0),
         lax.all_gather(part_out, "dp", axis=0, tiled=True),
         lax.all_gather(part_fc, "dp", axis=0, tiled=True),
         lax.all_gather(part_proj, "dp", axis=0, tiled=True),

time: 6410 us -> 7070 us (1.10)
  blocking collectives: 119 us -> 516 us
  waiting for transfers between devices: 4960 us -> 5090 us
  other arithmetic: 434 us -> 515 us
    unnamed x4, blocking collectives: 100 us -> 497 us
    unnamed x17, waiting for transfers between devices: 4160 us -> 4060 us
    ppermute x0 -> x3, waiting for transfers between devices: none -> 104 us  [gather_by_bits(): theirs = lax.ppermute(grown, axis, [(d, d ^ reach) for d in range(ways)])]
    all_gather x1, waiting for transfers between devices: 479 us -> 564 us  [local(): lax.all_gather(again_qkv, 'dp', axis=0, tiled=True)]
    all_gather x1 -> x2, other arithmetic: 325 us -> 362 us  [the longest x1 325 us: local(): lax.all_gather(again_qkv, 'dp', axis=0, tiled=True)]
    unnamed x101 -> x110, local copies, waits for them, and re-layouts: 152 us -> 159 us
  transfers between devices with their start and end apart: 13 -> 16, of which waited for: 8 -> 7; matrix products, arithmetic and copies ran while one was open for 15% -> 14% of each run, Pallas kernels for 0% -> 0%
where the time goes in v1:
time: 7070 us; the launch traced here: 7040 us
  waiting for transfers between devices  5090 us (72%)
  blocking collectives  516 us (7%)
  other arithmetic  515 us (7%)
  local copies, waits for them, and re-layouts  469 us (7%)
  matrix products  420 us (6%)
    unnamed x17, waiting for transfers between devices  4060 us
    all_gather x1, waiting for transfers between devices, local(): lax.all_gather(again_qkv, 'dp', axis=0, tiled=True)  564 us
    unnamed x4, blocking collectives  497 us
    all_gather x1, waiting for transfers between devices, local(): lax.all_gather(part_proj, 'dp', axis=0, tiled=True)  328 us
    all_gather x1, other arithmetic, local(): lax.all_gather(again_qkv, 'dp', axis=0, tiled=True)  325 us
    unnamed x110, local copies, waits for them, and re-layouts  159 us
  transfers between devices with their start and end apart: 16, of which 7 were waited for; matrix products, arithmetic and copies ran while one was open for 14% of the time, Pallas kernels for 0%

profile of v1, /device:TPU:0, one launch (start us, length us, event | category | flops | bytes accessed | tf_op | source)
XLA Modules:
  0.0 7040.6 jit_solution(6678895243366462060)
XLA Ops:
  13.5 35.3 all-gather.19.cloned.1.call-done
  48.8 37.1 reduce.24
  90.3 42.6 collective-permute-done
  174.0 61.5 collective-permute-done.1
  278.4 448.3 %all-reduce.22 = (bf16[6400]{0:T(1024)(128)(2,1)S(1)}, bf16[6400]{0:T(1024)(128)(2,1)S(1)}) all-reduce(bf16[6400]{0:T(1024)(128)(2,1)S(1)} %dynamic-update-slice.3, bf16[6400]{0:T(1024)(128)(2,1)S(1)} %dynamic-update-slice.1), channel_id=1, replica_groups=mesh['dp'=8,'seq'=4] {'dp'}, use_global_device_ids=true, to_apply=%add.3 | all-reduce | flops 12800 | bytes 51200
  804.5 39.9 dynamic-update-slice.5
  868.1 31.8 reduce.26
  937.7 80.0 %while.28 = (s32[]{:T(128)}, bf16[25,1,256,64]{2,3,1,0:T(8,128)(2,1)S(1)}, f32[25,1,256]{2,1,0:T(1,128)S(1)}, bf16[25,1,256,64]{3,2,1,0:T(8,128)(2,1)}, bf16[25,...) while((s32[]{:T(128)}, ...), condition=%wide.region_5.6_spmd.clone, body=%wide.region_2.5_spmd.clone.sunk | while | flops 69730048 | bytes 3815529 | solution.py:143
  1023.2 447.7 %all-reduce.31.cloned.1.call-done = bf16[10246400]{0:T(1024)(128)(2,1)} async-done(((bf16[10246400]{0:T(1024)(128)(2,1)}), bf16[10246400]{0:T(1024)(128)(2,1)}) %all-reduce.31.cloned.1.call-update) | async-done | bytes 20492816
  1488.0 35.3 slice.74
  1536.4 327.7 %all-gather.17.cloned.1.call-done = bf16[10240000]{0:T(1024)(128)(2,1)} async-done(((bf16[1280000]{0:T(1024)(128)(2,1)}), bf16[10240000]{0:T(1024)(128)(2,1)}) %all-gather.17.cloned.1.call-update) | async-done | bytes 20480016 | tf_op jit(solution)/shard_map/all_gather | solution.py:110
  1864.2 33.9 reshape.558
  1933.7 200.9 %while.29 = (s32[]{:T(128)}, bf16[25,1,256,64]{2,3,1,0:T(8,128)(2,1)S(1)}, f32[25,1,1024,64]{2,3,1,0:T(8,128)}, f32[25,1,1024,64]{2,3,1,0:T(8,128)}, bf16[25,1,2...) while((s32[]{:T(128)}, ...), condition=%wide.region_12.13_spmd.clone, body=%wide.region_10.12_spmd.clone.sunk | while | flops 171179776 | bytes 9515137 | solution.py:220
  2135.2 22.7 fusion.92
  2157.9 48.4 reshape.569
  2245.3 28.0 pad_maximum_fusion
  2273.3 39.9 reshape.568
  2329.9 36.6 reshape.566
  2369.3 3608.9 %all-reduce.33.cloned.1.call-done = (f32[7680000]{0:T(1024)}, f32[2560000]{0:T(1024)}, f32[10246400]{0:T(1024)}, f32[10240000]{0:T(1024)}) async-done(((f32[7680000]{0:T(1024)}, f32[2560000]{0:T(1024)}, f32[10246400]{0:T(1024)}, f32[10240000]{0:T(1024)}), (f32[7680000]{0:T(1024)}, f32[2560000]{0:T(1024)}, f32[10246400]{0:T(1024)}, f32[10240000]{0:T(1024)})) %all-reduce.33.cloned.1.call-update) | async-done | bytes 122905616
  5999.2 564.3 %all-gather.25.cloned.1.call-done = bf16[8,1,960000]{2,1,0:T(2,128)(2,1)} async-done(((bf16[1,1,960000]{2,1,0:T(2,128)(2,1)}), bf16[8,1,960000]{2,1,0:T(2,128)(2,1)}) %all-gather.25.cloned.1.call-update) | async-done | bytes 15360016 | tf_op jit(solution)/shard_map/all_gather | solution.py:175
  6563.5 325.4 %reduce.28 = bf16[8,960000]{1,0:T(8,128)(2,1)} reduce(bf16[8,1,960000]{2,1,0:T(2,128)(2,1)} %all-gather.25.cloned.1.call-done, bf16[]{:T(256)} %constant.183), dimensions={1}, to_apply=%all-gather.4.reduce_sub_computation | reduce | bytes 30720002 | tf_op jit(solution)/shard_map/all_gather | solution.py:175
  6888.8 33.8 reshape.645
  6922.7 25.2 reshape.565
  6977.1 36.4 all-reduce.18
  (513 shorter events, 704.5 us)
Async XLA Ops:
  7.2 41.6 all-gather.19.cloned.1.call-start
  13.4 783.7 %all-reduce.29.cloned.1.call-start = ((), (), s32[]{:S(2)}) async-start(), calls=%async_computation.7 | async-start | bytes 5124096
  88.7 66.5 copy-start.4
  88.8 44.2 collective-permute-start
  150.9 84.6 %collective-permute-start.1 = (bf16[1920000]{0:T(1024)(128)(2,1)}, bf16[1920000]{0:T(1024)(128)(2,1)}, u32[]{:S(2)}, u32[]{:S(2)}) collective-permute-start(bf16[1920000]{0:T(1024)(128)(2,1)} %maximum_select_fusion.7), channel_id=1, source_target_pairs={{0,8},{4,12},{8,0},{12,4},{16,24},{20,28},{24,16},{28,20},{1,9},{5... | collective-permute-start | bytes 11520008 | tf_op jit(solution)/shard_map/ppermute | solution.py:15
  165.8 678.7 %all-gather.23.cloned.1.call-start = ((), (), s32[]{:S(2)}) async-start(), calls=%async_computation.11 | async-start | bytes 6400000 | tf_op jit(solution)/shard_map/all_gather | solution.py:102
  173.9 694.1 %all-gather.21.cloned.1.call-start = ((), (), s32[]{:S(2)}) async-start(), calls=%async_computation.10 | async-start | bytes 11520000 | tf_op jit(solution)/shard_map/all_gather | solution.py:108
  174.0 76.8 %copy-start.18 = (bf16[80000]{0:T(1024)(128)(2,1)S(1)}, bf16[80000]{0:T(1024)(128)(2,1)}, u32[]{:S(2)}) copy-start(bf16[80000]{0:T(1024)(128)(2,1)} %param.17) | copy-start | bytes 480004
  174.0 97.1 %copy-start.37 = (bf16[200]{0:T(256)(128)(2,1)S(1)}, bf16[200]{0:T(256)(128)(2,1)}, u32[]{:S(2)}) copy-start(bf16[200]{0:T(256)(128)(2,1)} %param.21) | copy-start | bytes 1204
  174.0 97.3 %copy-start.38 = (bf16[200]{0:T(256)(128)(2,1)S(1)}, bf16[200]{0:T(256)(128)(2,1)}, u32[]{:S(2)}) copy-start(bf16[200]{0:T(256)(128)(2,1)} %param.20) | copy-start | bytes 1204
  248.0 478.7 %copy-start.2 = (bf16[1,256,1600]{1,2,0:T(8,128)(2,1)S(1)}, bf16[1,256,1600]{1,2,0:T(8,128)(2,1)}, u32[]{:S(2)}) copy-start(bf16[1,256,1600]{1,2,0:T(8,128)(2,1)} %param.13) | copy-start | bytes 2457604
  248.0 511.9 %collective-permute-start.2 = (bf16[3840000]{0:T(1024)(128)(2,1)}, bf16[3840000]{0:T(1024)(128)(2,1)}, u32[]{:S(2)}, u32[]{:S(2)}) collective-permute-start(bf16[3840000]{0:T(1024)(128)(2,1)} %maximum_select_fusion.3), channel_id=1, source_target_pairs={{0,16},{4,20},{8,24},{12,28},{16,0},{20,4},{24,8},{28,12},{1,17},{... | collective-permute-start | bytes 23040008 | tf_op jit(solution)/shard_map/ppermute | solution.py:15
  269.7 653.8 %all-gather.13.cloned.1.call-start = ((), (), s32[]{:S(2)}) async-start(), calls=%async_computation.2 | async-start | bytes 4096000 | tf_op jit(solution)/shard_map/all_gather | solution.py:137
  793.0 137.6 %all-gather.15.cloned.1.call-start = ((), (), s32[]{:S(2)}) async-start(), calls=%async_computation.3 | async-start | bytes 4096000 | tf_op jit(solution)/shard_map/all_gather | solution.py:138
  796.4 674.5 %all-reduce.31.cloned.1.call-start = ((), (), s32[]{:S(2)}) async-start(), calls=%async_computation.8 | async-start | bytes 40988672
  844.4 1019.8 %all-gather.17.cloned.1.call-start = ((), (), s32[]{:S(2)}) async-start(), calls=%async_computation.4 | async-start | bytes 23040000 | tf_op jit(solution)/shard_map/all_gather | solution.py:110
  867.2 1446.0 %reduce-scatter.3.cloned.1.call-start = ((), (), s32[]{:S(2)}) async-start(), calls=%async_computation.5 | async-start | bytes 8192000 | tf_op jit(solution)/shard_map/reduce_scatter | solution.py:225
  868.0 1267.2 %copy-start.33 = (bf16[256]{0:T(256)(128)(2,1)}, bf16[256]{0:T(256)(128)(2,1)S(1)}, u32[]{:S(2)}) copy-start(bf16[256]{0:T(256)(128)(2,1)S(1)} %compare_convert_fusion) | copy-start | bytes 1540
  1022.9 1204.0 %copy-start = (f32[1,256,1600]{1,2,0:T(8,128)}, f32[1,256,1600]{1,2,0:T(8,128)S(1)}, u32[]{:S(2)}) copy-start(f32[1,256,1600]{1,2,0:T(8,128)S(1)} %get-tuple-element.235) | copy-start | bytes 4915204
  1536.4 361.7 %copy-start.6 = (bf16[1,256,1600]{1,2,0:T(8,128)(2,1)S(1)}, bf16[1,256,1600]{1,2,0:T(8,128)(2,1)}, u32[]{:S(2)}) copy-start(bf16[1,256,1600]{1,2,0:T(8,128)(2,1)} %param.14) | copy-start | bytes 2457604
  2134.6 180.3 %reduce-scatter.5.cloned.1.call-start = ((), (), s32[]{:S(2)}) async-start(), calls=%async_computation.6 | async-start | bytes 8192000 | tf_op jit(solution)/shard_map/reduce_scatter | solution.py:226
  2135.2 3843.0 %all-reduce.33.cloned.1.call-start = ((), (), s32[]{:S(2)}) async-start(), calls=%async_computation.13 | async-start | bytes 245817344
  2366.4 4197.0 %all-gather.25.cloned.1.call-start = ((), (), s32[]{:S(2)}) async-start(), calls=%async_computation.12 | async-start | bytes 34560000 | tf_op jit(solution)/shard_map/all_gather | solution.py:175
  2367.0 4657.0 %all-reduce.35.cloned.1.call-start = ((), (), s32[]{:S(2)}) async-start(), calls=%async_computation.14 | async-start | bytes 30736384
  (31 other events, 787.3 us)
Sparse Core Ops, SparseCore 0:
  13.6 35.1 all-gather.18
  165.9 58.3 all-reduce.28
  226.5 46.5 all-gather.22
  275.4 334.5 all-gather.20
  793.1 27.7 all-gather.12
  823.0 29.7 all-gather.14
  857.4 613.4 all-reduce.30
  1472.5 391.6 all-gather.16
  2134.7 60.0 reduce-scatter.2
  2197.2 60.0 reduce-scatter.4
  2366.5 3611.5 all-reduce.32
  5979.6 583.8 all-gather.24
  6566.8 267.0 all-reduce.34
